TPU v7x, 32 devices: a whole 2x2x4 slice. The times are simulated.
32 devices in a mesh: section: 4 (over y, core), seq: 8 (over z, x).
Axes of the slice: x: 2, y: 2, z: 4, core: 2. Of those that a mesh axis runs over, the one named last changes fastest.
Arguments:
- pending_residual: bfloat16 [4, 4096, 1536], P('section', 'seq'), may hold values from -32 to 32
- intragroup_mixing_matrix: bfloat16 [4, 8, 512, 512], P('section', 'seq'), may hold values from -0.25 to 0.25
- intergroup_mixing_matrix: bfloat16 [4, 512, 8, 8], P('section', 'seq'), may hold values from -2 to 2
- token_rescale_factor: float32 [4, 1536], P('section'), may hold values from 0.1 to 1.9
- gating_diagonal_matrix: bfloat16 [4, 1536, 768], P('section', 'seq'), may hold values from -0.3125 to 0.3125
- expanding_diagonal_matrix: bfloat16 [4, 1536, 768], P('section', 'seq'), may hold values from -0.3125 to 0.3125
- contracting_diagonal_matrix: bfloat16 [4, 3072, 384], P('section', 'seq'), may hold values from -0.21875 to 0.21875
- feature_rescale_factor: float32 [4, 1536], P('section'), may hold values from 0.1 to 1.9
Outputs:
- advanced: bfloat16 [4, 4096, 1536], P('section', 'seq')
All inputs are finite; a program needn't handle non-finite values.
Results may differ from a plain program's by a relative error of at most 0.0051.
Values may be sent and summed in bfloat16 or wider, within the bound.
A program may use at most 64 MiB of HBM per device.

v0:
```python
import jax
import jax.numpy as jnp
from jax import lax
from jax.sharding import PartitionSpec as P

D = 1536
FF = 3072
NB = 4
B1 = 512


def from_behind(value, axis, by):
    size = lax.axis_size(axis)
    return lax.ppermute(value, axis, [(i, (i + by) % size) for i in range(size)])


def rms_norm(values, gain):
    scale = lax.rsqrt(jnp.mean(values * values, axis=-1, keepdims=True) + 1e-06)
    return values * scale * gain


def shards(
    pending_residual,
    intragroup_mixing_matrix,
    intergroup_mixing_matrix,
    token_rescale_factor,
    gating_diagonal_matrix,
    expanding_diagonal_matrix,
    contracting_diagonal_matrix,
    feature_rescale_factor,
):
    resident_tokens = pending_residual.shape[1]
    groups_here = resident_tokens // B1
    activation_vector = pending_residual[0].astype(jnp.float32)
    normed = (
        rms_norm(activation_vector, token_rescale_factor[0])
        .astype(jnp.bfloat16)
        .reshape(groups_here, B1, D)
    )
    mixed = jnp.einsum(
        "aob,abc->aoc", intragroup_mixing_matrix[0], normed, preferred_element_type=jnp.float32
    ).astype(jnp.bfloat16)
    moved = lax.all_to_all(mixed, "seq", split_axis=1, concat_axis=0, tiled=True)
    turned = jnp.einsum(
        "oae,eoc->aoc", intergroup_mixing_matrix[0], moved, preferred_element_type=jnp.float32
    ).astype(jnp.bfloat16)
    returned = lax.all_to_all(turned, "seq", split_axis=0, concat_axis=1, tiled=True)
    merged = activation_vector + returned.reshape(resident_tokens, D).astype(jnp.float32)
    normed_mlp = (
        rms_norm(merged, feature_rescale_factor[0]).astype(jnp.bfloat16).reshape(-1, NB, D // NB)
    )
    gate_all, up_all = (
        lax.all_gather(gating_diagonal_matrix[0], "seq", axis=0, tiled=True),
        lax.all_gather(expanding_diagonal_matrix[0], "seq", axis=0, tiled=True),
    )
    gate_proj = jnp.einsum(
        "tkd,kdf->tkf",
        normed_mlp,
        gate_all.reshape(NB, D // NB, FF // NB),
        preferred_element_type=jnp.float32,
    )
    up_proj = jnp.einsum(
        "tkd,kdf->tkf",
        normed_mlp,
        up_all.reshape(NB, D // NB, FF // NB),
        preferred_element_type=jnp.float32,
    )
    hidden = (jax.nn.silu(gate_proj) * up_proj).astype(jnp.bfloat16)
    down_all = lax.all_gather(contracting_diagonal_matrix[0], "seq", axis=0, tiled=True)
    lowered = jnp.einsum(
        "tkf,kfe->tke",
        hidden,
        down_all.reshape(NB, FF // NB, D // NB),
        preferred_element_type=jnp.float32,
    )
    layer_out = (merged + lowered.reshape(-1, D)).astype(jnp.bfloat16)
    shifted = from_behind(layer_out, "section", 1)
    return shifted[None]


def solution(mesh):
    return jax.shard_map(
        shards,
        mesh=mesh,
        in_specs=(
            P("section", "seq", None),
            P("section", "seq", None, None),
            P("section", "seq", None, None),
            P("section", None),
            P("section", "seq", None),
            P("section", "seq", None),
            P("section", "seq", None),
            P("section", None),
        ),
        out_specs=P("section", "seq", None),
        check_vma=False,
    )
```

profile of v0, /device:TPU:11, one launch (start us, length us, event | category | flops | bytes accessed | tf_op | source)
XLA Modules:
  0.0 257.0 jit_solution(6573348122779553789)
XLA Ops:
  6.5 0.0 copy-start
  6.5 0.0 all-gather.7.cloned.1.call-start
  6.5 0.7 all-gather.7.cloned.1.call-update
  7.3 0.0 all-gather.9.cloned.1.call-start
  7.3 0.7 all-gather.9.cloned.1.call-update
  8.0 0.7 reduce
  8.7 1.8 fusion.4
  10.5 0.0 copy-done
  10.5 2.6 %fusion.8 = bf16[1,512,1536]{1,2,0:T(8,128)(2,1)S(1)} fusion(bf16[1,512,1536]{2,1,0:T(8,128)(2,1)} %param.8, f32[1536]{0:T(1024)S(1)} %reduce, f32[512]{0:T(512)S(1)} %add_rsqrt_fusion.1, bf16[1,1,512,512]{3,2,1,0:T(8,128)(2,1)S(1)} %copy-done), kind=kOutput, calls=%fused_computation.18 | convolution fusion | flops 809238528 | bytes 3678208 | tf_op jit(solution)/shard_map/aob,abc->aoc/dot_general | solution.py:40
  13.1 5.8 %copy.21 = bf16[1,512,1536]{2,0,1:T(2,128)(2,1)} copy(bf16[1,512,1536]{1,2,0:T(8,128)(2,1)S(1)} %fusion.8) | data formatting | bytes 3145728 | tf_op jit(solution)/shard_map/convert_element_type | solution.py:42
  19.0 0.5 broadcast.51
  19.5 11.2 %reduce.2 = bf16[512,1536]{1,0:T(8,128)(2,1)S(1)} reduce(bf16[512,1,1536]{2,1,0:T(2,128)(2,1)} %bitcast.61, bf16[]{:T(256)} %broadcast.51), dimensions={1}, to_apply=%bitcast.55.reduce_sub_computation | reduce | bytes 3145730
  30.7 2.4 reshape.99
  33.1 0.0 copy-start.3
  33.1 5.8 %all-to-all-start = ((bf16[8,2,49152]{2,1,0:T(2,128)(2,1)}), bf16[8,2,49152]{2,1,0:T(2,128)(2,1)S(1)}, u32[]{:S(2)}, u32[]{:S(2)}) async-start(bf16[8,2,49152]{2,1,0:T(2,128)(2,1)} %reshape.99), calls=%async_computation | async-start | bytes 3145728 | tf_op jit(solution)/shard_map/all_to_all | solution.py:43
  38.9 0.0 copy-done.3
  38.9 0.1 copy.23
  39.1 52.0 %all-to-all-done = bf16[8,2,49152]{2,1,0:T(2,128)(2,1)S(1)} async-done(((bf16[8,2,49152]{2,1,0:T(2,128)(2,1)}), bf16[8,2,49152]{2,1,0:T(2,128)(2,1)S(1)}, u32[]{:S(2)}, u32[]{:S(2)}) %all-to-all-start) | async-done | bytes 1572896 | tf_op jit(solution)/shard_map/all_to_all | solution.py:43
  91.0 4.0 %reshape.100 = bf16[512,1,1536]{2,1,0:T(2,128)(2,1)} reshape(bf16[8,2,49152]{2,1,0:T(2,128)(2,1)S(1)} %all-to-all-done) | data formatting | bytes 3145728
  95.0 2.4 copy.30
  97.4 1.0 fusion.7
  98.4 1.6 copy.24
  100.0 0.0 copy-start.1
  100.0 7.1 %all-to-all-start.1 = ((bf16[8,64,1536]{2,1,0:T(8,128)(2,1)}), bf16[8,64,1536]{2,1,0:T(8,128)(2,1)}, u32[]{:S(2)}, u32[]{:S(2)}) async-start(bf16[8,64,1536]{2,1,0:T(8,128)(2,1)} %copy.24), calls=%async_computation.1 | async-start | bytes 3145728 | tf_op jit(solution)/shard_map/all_to_all | solution.py:47
  107.1 0.0 all-gather.11.cloned.1.call-start
  107.1 0.7 all-gather.11.cloned.1.call-update
  107.9 0.0 copy-done.1
  107.9 0.0 copy-start.4
  107.9 2.2 reshape.89
  110.0 0.0 copy-done.4
  110.1 50.5 %all-to-all-done.1 = bf16[8,64,1536]{2,1,0:T(8,128)(2,1)} async-done(((bf16[8,64,1536]{2,1,0:T(8,128)(2,1)}), bf16[8,64,1536]{2,1,0:T(8,128)(2,1)}, u32[]{:S(2)}, u32[]{:S(2)}) %all-to-all-start.1) | async-done | bytes 1572896 | tf_op jit(solution)/shard_map/all_to_all | solution.py:47
  160.6 4.3 %reshape.90 = f32[512,4,384]{2,1,0:T(4,128)} reshape(bf16[8,64,1536]{2,1,0:T(8,128)(2,1)} %all-to-all-done.1) | data formatting | bytes 4718592 | tf_op jit(solution)/shard_map/convert_element_type | solution.py:48
  164.9 0.0 copy-start.2
  164.9 2.1 multiply_reduce_fusion
  167.1 0.2 copy-done.2
  167.3 3.9 %multiply_convert_fusion = bf16[512,4,384]{2,1,0:T(4,128)(2,1)} fusion(f32[512,4,384]{2,1,0:T(4,128)S(1)} %copy-done.2, f32[512,4,384]{2,1,0:T(4,128)} %reshape.90, f32[4,384]{1,0:T(4,128)S(1)} %mul.62, f32[512]{0:T(512)S(1)} %add_rsqrt_fusion), kind=kLoop, calls=%fused_computation.11 | loop fusion | flops 3145728 | bytes 7872512 | tf_op jit(solution)/shard_map/convert_element_type | solution.py:50
  171.2 0.0 all-gather.7.cloned.1.call-done
  171.2 6.7 %fusion.18 = f32[4,512,768]{2,1,0:T(8,128)} fusion(bf16[4,384,768]{2,1,0:T(8,128)(2,1)} %bitcast.65, bf16[512,4,384]{2,1,0:T(4,128)(2,1)} %multiply_convert_fusion), kind=kOutput, calls=%fused_computation.25 | convolution fusion | flops 1207959552 | bytes 10223616 | tf_op jit(solution)/shard_map/tkd,kdf->tkf/dot_general | solution.py:56
  177.9 0.0 all-gather.9.cloned.1.call-done
  177.9 34.9 %all-gather.11.cloned.1.call-done = bf16[1,3072,384]{2,1,0:T(8,128)(2,1)} async-done(((bf16[1,384,384]{2,1,0:T(8,128)(2,1)}), bf16[1,3072,384]{2,1,0:T(8,128)(2,1)}) %all-gather.11.cloned.1.call-update) | async-done | bytes 2359312 | tf_op jit(solution)/shard_map/all_gather | solution.py:69
  212.9 9.7 %fusion.5 = f32[4,512,384]{1,2,0:T(8,128)} fusion(bf16[4,768,384]{2,1,0:T(8,128)(2,1)} %bitcast.69, f32[4,512,768]{2,1,0:T(8,128)} %fusion.18, bf16[4,384,768]{2,1,0:T(8,128)(2,1)} %bitcast.68, bf16[512,4,384]{2,1,0:T(4,128)(2,1)} %multiply_convert_fusion), kind=kOutput, calls=%fused_computation.14 | convolution fusion | flops 2425356288 | bytes 15728640 | tf_op jit(solution)/shard_map/tkf,kfe->tke/dot_general | solution.py:70
  222.6 3.5 %copy.28 = f32[512,1536]{1,0:T(8,128)} copy(f32[512,1536]{0,1:T(8,128)} %bitcast.64) | data formatting | bytes 6291456 | tf_op jit(solution)/shard_map/reshape | solution.py:76
  226.1 3.0 %add_convert_fusion = bf16[512,1536]{1,0:T(8,128)(2,1)S(1)} fusion(f32[512,1536]{1,0:T(8,128)} %copy.28, bf16[1,512,1536]{2,1,0:T(8,128)(2,1)S(1)} %copy-done.1, bf16[8,64,1536]{2,1,0:T(8,128)(2,1)} %all-to-all-done.1), kind=kLoop, calls=%fused_computation.10 | loop fusion | flops 3932160 | bytes 7864320 | tf_op jit(solution)/shard_map/convert_element_type | solution.py:76
  229.1 2.9 %collective-permute-start = (bf16[512,1536]{1,0:T(8,128)(2,1)S(1)}, bf16[512,1536]{1,0:T(8,128)(2,1)S(1)}, u32[]{:S(2)}, u32[]{:S(2)}) collective-permute-start(bf16[512,1536]{1,0:T(8,128)(2,1)S(1)} %add_convert_fusion), channel_id=1, source_target_pairs={{0,8},{8,16},{16,24},{24,0},{1,9},{9,17},{17,25},{25,1},{2,10},{10... | collective-permute-start | bytes 4718600 | tf_op jit(solution)/shard_map/ppermute | solution.py:14
  232.0 17.4 %collective-permute-done = bf16[512,1536]{1,0:T(8,128)(2,1)S(1)} collective-permute-done((bf16[512,1536]{1,0:T(8,128)(2,1)S(1)}, bf16[512,1536]{1,0:T(8,128)(2,1)S(1)}, u32[]{:S(2)}, u32[]{:S(2)}) %collective-permute-start) | collective-permute-done | bytes 1572896 | tf_op jit(solution)/shard_map/ppermute | solution.py:14
  249.3 1.1 copy.39
  (4 shorter events, 0.0 us)
Async XLA Ops:
  6.5 4.0 %copy-start = (bf16[1,1,512,512]{3,2,1,0:T(8,128)(2,1)S(1)}, bf16[1,1,512,512]{3,2,1,0:T(8,128)(2,1)}, u32[]{:S(2)}) copy-start(bf16[1,1,512,512]{3,2,1,0:T(8,128)(2,1)} %param.9) | copy-start | bytes 1572868
  6.5 164.7 %all-gather.7.cloned.1.call-start = ((), (), s32[]{:S(2)}) async-start(), calls=%async_computation.2 | async-start | bytes 2654208 | tf_op jit(solution)/shard_map/all_gather | solution.py:53
  7.3 170.7 %all-gather.9.cloned.1.call-start = ((), (), s32[]{:S(2)}) async-start(), calls=%async_computation.3 | async-start | bytes 2654208 | tf_op jit(solution)/shard_map/all_gather | solution.py:54
  33.1 5.8 %copy-start.3 = (bf16[1,64,8,8]{1,3,2,0:T(8,128)(2,1)S(1)}, bf16[1,64,8,8]{1,3,2,0:T(8,128)(2,1)}, u32[]{:S(2)}) copy-start(bf16[1,64,8,8]{1,3,2,0:T(8,128)(2,1)} %param.10) | copy-start | bytes 24580
  33.1 57.9 %all-to-all-start = ((bf16[8,2,49152]{2,1,0:T(2,128)(2,1)}), bf16[8,2,49152]{2,1,0:T(2,128)(2,1)S(1)}, u32[]{:S(2)}, u32[]{:S(2)}) async-start(bf16[8,2,49152]{2,1,0:T(2,128)(2,1)} %reshape.99), calls=%async_computation | async-start | bytes 3145728 | tf_op jit(solution)/shard_map/all_to_all | solution.py:43
  100.0 7.8 %copy-start.1 = (bf16[1,512,1536]{2,1,0:T(8,128)(2,1)S(1)}, bf16[1,512,1536]{2,1,0:T(8,128)(2,1)}, u32[]{:S(2)}) copy-start(bf16[1,512,1536]{2,1,0:T(8,128)(2,1)} %param.8) | copy-start | bytes 4718596
  100.0 60.6 %all-to-all-start.1 = ((bf16[8,64,1536]{2,1,0:T(8,128)(2,1)}), bf16[8,64,1536]{2,1,0:T(8,128)(2,1)}, u32[]{:S(2)}, u32[]{:S(2)}) async-start(bf16[8,64,1536]{2,1,0:T(8,128)(2,1)} %copy.24), calls=%async_computation.1 | async-start | bytes 3145728 | tf_op jit(solution)/shard_map/all_to_all | solution.py:47
  107.1 105.7 %all-gather.11.cloned.1.call-start = ((), (), s32[]{:S(2)}) async-start(), calls=%async_computation.4 | async-start | bytes 2654208 | tf_op jit(solution)/shard_map/all_gather | solution.py:69
  107.9 2.2 copy-start.4
  164.9 2.4 copy-start.2
  229.1 20.2 %collective-permute-start = (bf16[512,1536]{1,0:T(8,128)(2,1)S(1)}, bf16[512,1536]{1,0:T(8,128)(2,1)S(1)}, u32[]{:S(2)}, u32[]{:S(2)}) collective-permute-start(bf16[512,1536]{1,0:T(8,128)(2,1)S(1)} %add_convert_fusion), channel_id=1, source_target_pairs={{0,8},{8,16},{16,24},{24,0},{1,9},{9,17},{17,25},{25,1},{2,10},{10... | collective-permute-start | bytes 4718600 | tf_op jit(solution)/shard_map/ppermute | solution.py:14
Sparse Core Ops, SparseCore 0:
  9.5 70.3 all-gather.6
  82.1 74.7 all-gather.8
  159.1 53.7 all-gather.10
where the time goes:
time: 261 us; the launch traced here: 257 us
  waiting for transfers between devices  157 us (60%)
  local copies, waits for them, and re-layouts  28.2 us (11%)
  other arithmetic  22.8 us (9%)
  matrix products  20.1 us (8%)
  starting transfers between devices  15.8 us (6%)
  between operations  13.2 us (5%)
    all_to_all x1, waiting for transfers between devices, shards(): lax.all_to_all(mixed, 'seq', split_axis=1, concat_axis=0, tiled=True)  52 us
    all_to_all x1, waiting for transfers between devices, shards(): lax.all_to_all(turned, 'seq', split_axis=0, concat_axis=1, tiled=True)  50.5 us
    all_gather x1, waiting for transfers between devices, shards(): lax.all_gather(contracting_diagonal_matrix[0], 'seq', axis=0, tiled=True)  34.9 us
    ppermute x1, waiting for transfers between devices, from_behind(): lax.ppermute(value, axis, [(i, (i + by) % size) for i in range(size)])  17.4 us
    unnamed x3, other arithmetic  12 us
    unnamed x15, local copies, waits for them, and re-layouts  10.6 us
    dot_general x1, matrix products, shards(): jnp.einsum('tkf,kfe->tke', hidden, down_all.reshape(NB, FF // NB, D // NB...  9.75 us
    all_to_all x1, starting transfers between devices, shards(): lax.all_to_all(turned, 'seq', split_axis=0, concat_axis=1, tiled=True)  7.12 us
  transfers between devices with their start and end apart: 6, of which 4 were waited for; matrix products, arithmetic and copies ran while one was open for 21% of the time, Pallas kernels for 0%

commit v1 on v0

v1 whole, which is shorter than its diff:
```python
import functools

import jax
import jax.numpy as jnp
from jax import lax
from jax.experimental import pallas as pl
from jax.experimental.pallas import tpu as pltpu
from jax.sharding import PartitionSpec as P

NB = 4
B1 = 512
CHUNKS = 4
AHEAD = 2
EPS = 1e-06
MESH = pl.DeviceIdType.MESH


def layer_kernel(
    n, sections, D, FF,
    x_ref, a_ref, w_ref, g1_ref, gate_ref, up_ref, down_ref, g2_ref,
    out_ref,
    normed, mixed, xr, mr, w2, w3, wg, wu, wd, merged, st, outs,
    xs, xrs, ms, mrs, os_, ors, ws, wrs, ts, trs, vs, vrs,
):
    q = n // NB
    R = B1 // q
    r = R // CHUNKS
    FB, FH = D // NB, FF // NB
    own_offsets = B1 // n
    me = lax.axis_index("seq")
    sec = lax.axis_index("section")
    k, h = me // q, me % q
    after = (sec + 1) % sections
    before = (sec + sections - 1) % sections

    barrier = pltpu.get_barrier_semaphore()

    def greet(j, carry):
        pl.semaphore_signal(barrier, inc=1, device_id=(after, j), device_id_type=MESH)
        pl.semaphore_signal(barrier, inc=1, device_id=(before, j), device_id_type=MESH)
        return carry

    def greet_peer(d, carry):
        j = (me + d) % n
        pl.semaphore_signal(barrier, inc=1, device_id=(sec, j), device_id_type=MESH)
        return carry

    lax.fori_loop(1, n, greet_peer, 0)
    lax.fori_loop(0, n, greet, 0)

    def block_of(ref, c, j):
        rows = pl.multiple_of((j % q) * R + c * r, r)
        cols = pl.multiple_of((j // q) * FB, FB)
        return ref.at[pl.ds(rows, r), pl.ds(cols, FB)]

    def slot(ref, c, j):
        return ref.at[c, pl.ds(pl.multiple_of(j * r, r), r), :]

    def spread(src, land, send, recv, c, j):
        return pltpu.make_async_remote_copy(
            src_ref=block_of(src, c, j), dst_ref=slot(land, c, me),
            send_sem=send.at[c, j], recv_sem=recv.at[c, me],
            device_id=(sec, j), device_id_type=MESH,
        )

    def arrival(land, send, recv, c, j):
        return pltpu.make_async_remote_copy(
            src_ref=slot(land, c, j), dst_ref=slot(land, c, j),
            send_sem=send.at[c, j], recv_sem=recv.at[c, j],
            device_id=(sec, j), device_id_type=MESH,
        )

    def keep(src, land, recv, c):
        return pltpu.make_async_copy(block_of(src, c, me), slot(land, c, me), recv.at[c, me])

    def start_chunk(src, land, send, recv, c):
        def one(d, carry):
            spread(src, land, send, recv, c, (me + d) % n).start()
            return carry

        lax.fori_loop(1, n, one, 0)
        keep(src, land, recv, c).start()

    def await_chunk(src, land, send, recv, c):
        def one(d, carry):
            arrival(land, send, recv, c, (me + d) % n).wait_recv()
            return carry

        lax.fori_loop(1, n, one, 0)
        keep(src, land, recv, c).wait()

    weights = ((gate_ref, wg, FB // q), (up_ref, wu, FB // q), (down_ref, wd, FH // q))

    def weight_copy(i, d):
        src, land, rows = weights[i]
        j = k * q + (h + d) % q
        return pltpu.make_async_remote_copy(
            src_ref=src, dst_ref=land.at[pl.ds(pl.multiple_of(h * rows, rows), rows), :],
            send_sem=ws.at[i, (h + d) % q], recv_sem=wrs.at[i, h],
            device_id=(sec, j), device_id_type=MESH,
        )

    def weight_arrival(i, d):
        src, land, rows = weights[i]
        p = (h + d) % q
        view = land.at[pl.ds(pl.multiple_of(p * rows, rows), rows), :]
        return pltpu.make_async_remote_copy(
            src_ref=view, dst_ref=view, send_sem=ws.at[i, p], recv_sem=wrs.at[i, p],
            device_id=(sec, k * q + p), device_id_type=MESH,
        )

    def weight_keep(i):
        src, land, rows = weights[i]
        return pltpu.make_async_copy(
            src, land.at[pl.ds(pl.multiple_of(h * rows, rows), rows), :], wrs.at[i, h]
        )

    def across_view(i):
        return w2.at[pl.ds(pl.multiple_of(i * own_offsets, own_offsets), own_offsets), :]

    def across_copy(b):
        return pltpu.make_async_remote_copy(
            src_ref=w_ref, dst_ref=across_view(me % NB),
            send_sem=vs.at[b], recv_sem=vrs.at[me % NB],
            device_id=(sec, b * q + me // NB), device_id_type=MESH,
        )

    def across_arrival(i):
        return pltpu.make_async_remote_copy(
            src_ref=across_view(i), dst_ref=across_view(i),
            send_sem=vs.at[i], recv_sem=vrs.at[i],
            device_id=(sec, h * NB + i), device_id_type=MESH,
        )

    def across_keep():
        return pltpu.make_async_copy(w_ref, across_view(me % NB), vrs.at[me % NB])

    def stat_copy(c, d):
        b = (k + d) % NB
        return pltpu.make_async_remote_copy(
            src_ref=st.at[c, k], dst_ref=st.at[c, k],
            send_sem=ts.at[c, b], recv_sem=trs.at[c, k],
            device_id=(sec, b * q + h), device_id_type=MESH,
        )

    def stat_arrival(c, d):
        b = (k + d) % NB
        return pltpu.make_async_remote_copy(
            src_ref=st.at[c, b], dst_ref=st.at[c, b],
            send_sem=ts.at[c, b], recv_sem=trs.at[c, b],
            device_id=(sec, b * q + h), device_id_type=MESH,
        )

    def out_view(c, j):
        rows = pl.multiple_of((j % q) * R + c * r, r)
        cols = pl.multiple_of((j // q) * FB, FB)
        return out_ref.at[pl.ds(rows, r), pl.ds(cols, FB)]

    def out_copy(c, j):
        return pltpu.make_async_remote_copy(
            src_ref=slot(outs, c, j), dst_ref=out_view(c, me),
            send_sem=os_.at[c, j], recv_sem=ors.at[c, me],
            device_id=(after, j), device_id_type=MESH,
        )

    def out_arrival(c, j):
        return pltpu.make_async_remote_copy(
            src_ref=slot(outs, c, j), dst_ref=out_view(c, j),
            send_sem=os_.at[c, j], recv_sem=ors.at[c, j],
            device_id=(before, j), device_id_type=MESH,
        )

    pl.semaphore_wait(barrier, 3 * n - 1)

    for b in range(NB):
        to = b * q + me // NB

        @pl.when(to != me)
        def _():
            across_copy(b).start()

        @pl.when(to == me)
        def _():
            across_keep().start()

    start_chunk(x_ref, xr, xs, xrs, 0)

    def norm_rows(i, carry):
        rows = pl.ds(pl.multiple_of(i * 64, 64), 64)
        v = x_ref[rows, :].astype(jnp.float32)
        scale = lax.rsqrt(jnp.sum(v * v, axis=-1, keepdims=True) * (1.0 / D) + EPS)
        normed[rows, :] = (v * scale * g1_ref[...]).astype(jnp.bfloat16)
        return carry

    lax.fori_loop(0, B1 // 64, norm_rows, 0)
    for b in range(NB):
        cols = slice(b * FB, (b + 1) * FB)
        mixed[:, cols] = jnp.dot(
            a_ref[...], normed[:, cols], preferred_element_type=jnp.float32
        ).astype(jnp.bfloat16)

    start_chunk(mixed, mr, ms, mrs, 0)
    for i in range(3):
        for d in range(1, q):
            weight_copy(i, d).start()
        weight_keep(i).start()
    for c in range(1, AHEAD):
        start_chunk(mixed, mr, ms, mrs, c)
        start_chunk(x_ref, xr, xs, xrs, c)

    for i in range(NB):
        come = h * NB + i

        @pl.when(come != me)
        def _():
            across_arrival(i).wait_recv()

        @pl.when(come == me)
        def _():
            across_keep().wait()

    for a in range(n):
        w3[a] = w2[:, a * n : (a + 1) * n].astype(jnp.float32)

    T = 16

    def turn_tile(c, i):
        rows = pl.multiple_of(i * T, T)

        def piece(e):
            return pl.ds(pl.multiple_of(e * r + rows, T), T)

        def weights_of(a):
            return w3[a, pl.ds(pl.multiple_of(c * r + rows, T), T), :]

        def finish(a, acc):
            v = xr[c, piece(a), :].astype(jnp.float32)
            v = v + acc.astype(jnp.bfloat16).astype(jnp.float32)
            merged[c, piece(a), :] = v

        if n <= 8:
            m = [mr[c, piece(e), :].astype(jnp.float32) for e in range(n)]
            for a in range(n):
                w = weights_of(a)
                acc = w[:, 0:1] * m[0]
                for e in range(1, n):
                    acc = acc + w[:, e : e + 1] * m[e]
                finish(a, acc)
        else:

            def one(a, carry):
                w = weights_of(a)
                acc = jnp.zeros((T, FB), jnp.float32)
                for e in range(n):
                    acc = acc + w[:, e : e + 1] * mr[c, piece(e), :].astype(jnp.float32)
                finish(a, acc)
                return carry

            lax.fori_loop(0, n, one, 0)

    def step(c, carry):
        @pl.when(c < CHUNKS)
        def _():
            await_chunk(mixed, mr, ms, mrs, c)
            await_chunk(x_ref, xr, xs, xrs, c)

            def tile(i, carry):
                turn_tile(c, i)
                return carry

            lax.fori_loop(0, r // T, tile, 0)
            v = merged[c]
            st[c, k] = lax.dot_general(
                jnp.ones((8, FB), jnp.float32), v * v, (((1,), (1,)), ((), ())),
                precision=lax.Precision.HIGHEST, preferred_element_type=jnp.float32,
            )
            for d in range(1, NB):
                stat_copy(c, d).start()

        @pl.when(c + AHEAD < CHUNKS)
        def _():
            start_chunk(mixed, mr, ms, mrs, c + AHEAD)
            start_chunk(x_ref, xr, xs, xrs, c + AHEAD)

        @pl.when(c == 1)
        def _():
            for i in range(3):
                for d in range(1, q):
                    weight_arrival(i, d).wait_recv()
                weight_keep(i).wait()

        @pl.when(c >= 1)
        def _():
            p = c - 1
            for d in range(1, NB):
                stat_arrival(p, d).wait_recv()
            total = (st[p, 0] + st[p, 1]) + (st[p, 2] + st[p, 3])
            scale = jnp.transpose(lax.rsqrt(total * (1.0 / D) + EPS))[:, 0:1]
            half = n * r // 2
            for t in range(2):
                rows = slice(t * half, (t + 1) * half)
                v = merged[p, rows, :]
                inner = (v * scale[rows] * g2_ref[...]).astype(jnp.bfloat16)
                gate = jnp.dot(inner, wg[...], preferred_element_type=jnp.float32)
                up = jnp.dot(inner, wu[...], preferred_element_type=jnp.float32)
                hidden = (gate / (1.0 + jnp.exp(-gate)) * up).astype(jnp.bfloat16)
                low = jnp.dot(hidden, wd[...], preferred_element_type=jnp.float32)
                outs[p, rows, :] = (v + low).astype(jnp.bfloat16)

            def one(d, carry):
                out_copy(p, (me + d) % n).start()
                return carry

            lax.fori_loop(0, n, one, 0)

        return carry

    lax.fori_loop(0, CHUNKS + 1, step, 0)

    for b in range(NB):

        @pl.when(b * q + me // NB != me)
        def _():
            across_copy(b).wait_send()

    for i in range(3):
        for d in range(1, q):
            weight_copy(i, d).wait_send()

    def drain(c, carry):
        def one(d, carry):
            j = (me + d) % n
            spread(x_ref, xr, xs, xrs, c, j).wait_send()
            spread(mixed, mr, ms, mrs, c, j).wait_send()
            return carry

        lax.fori_loop(1, n, one, 0)
        for d in range(1, NB):
            stat_copy(c, d).wait_send()

        def last(j, carry):
            out_copy(c, j).wait_send()
            out_arrival(c, j).wait_recv()
            return carry

        return lax.fori_loop(0, n, last, carry)

    lax.fori_loop(0, CHUNKS, drain, 0)


def shards(n, sections, pending, along, across, gain_one, gate, up, down, gain_two):
    D = pending.shape[2]
    FB = D // NB
    FH = gate.shape[2]
    FF = FH * NB
    q = n // NB
    R = B1 // q
    r = R // CHUNKS
    flat = across[0].reshape(B1 // n, n * n)
    lanes = max(n * n, 128)
    flat = jnp.pad(flat, ((0, 0), (0, lanes - n * n)))
    k = lax.axis_index("seq") // q
    gain_two = lax.dynamic_slice(gain_two, (0, k * FB), (1, FB))
    vmem = pl.BlockSpec(memory_space=pltpu.VMEM)
    anywhere = pl.BlockSpec(memory_space=pl.ANY)
    dma = pltpu.SemaphoreType.DMA
    bf, f32 = jnp.bfloat16, jnp.float32
    out = pl.pallas_call(
        functools.partial(layer_kernel, n, sections, D, FF),
        out_shape=jax.ShapeDtypeStruct((B1, D), bf),
        in_specs=[vmem, vmem, anywhere, vmem, anywhere, anywhere, anywhere, vmem],
        out_specs=anywhere,
        scratch_shapes=[
            pltpu.VMEM((B1, D), bf),
            pltpu.VMEM((B1, D), bf),
            pltpu.VMEM((CHUNKS, n * r, FB), bf),
            pltpu.VMEM((CHUNKS, n * r, FB), bf),
            pltpu.VMEM((R, lanes), bf),
            pltpu.VMEM((n, R, n), f32),
            pltpu.VMEM((FB, FH), bf),
            pltpu.VMEM((FB, FH), bf),
            pltpu.VMEM((FH, FB), bf),
            pltpu.VMEM((CHUNKS, n * r, FB), f32),
            pltpu.VMEM((CHUNKS, NB, 8, n * r), f32),
            pltpu.VMEM((CHUNKS, n * r, FB), bf),
            dma((CHUNKS, n)), dma((CHUNKS, n)),
            dma((CHUNKS, n)), dma((CHUNKS, n)),
            dma((CHUNKS, n)), dma((CHUNKS, n)),
            dma((3, q)), dma((3, q)),
            dma((CHUNKS, NB)), dma((CHUNKS, NB)),
            dma((NB,)), dma((NB,)),
        ],
        compiler_params=pltpu.CompilerParams(
            collective_id=0, has_side_effects=True, vmem_limit_bytes=48 * 1024 * 1024
        ),
        name="encoder_layer",
    )(pending[0], along[0, 0], flat, gain_one, gate[0], up[0], down[0], gain_two)
    return out[None]


def solution(mesh):
    return jax.shard_map(
        functools.partial(shards, mesh.shape["seq"], mesh.shape["section"]),
        mesh=mesh,
        in_specs=(
            P("section", "seq", None),
            P("section", "seq", None, None),
            P("section", "seq", None, None),
            P("section", None),
            P("section", "seq", None),
            P("section", "seq", None),
            P("section", "seq", None),
            P("section", None),
        ),
        out_specs=P("section", "seq", None),
        check_vma=False,
    )
```

time: 261 us -> 126 us (0.48); the launches traced: 257 us -> 125 us
  waiting for transfers between devices: 157 us -> 0 us
  Pallas kernels: 0 us -> 117 us
  other arithmetic: 22.8 us -> 0 us
  matrix products: 20.1 us -> 0 us
  local copies, waits for them, and re-layouts: 28.2 us -> 8.67 us
  starting transfers between devices: 15.8 us -> 0 us
  between operations: 13.2 us -> 0.03 us
    pallas_call x0 -> x1, Pallas kernels: none -> 117 us  [shards(): pl.pallas_call(functools.partial(layer_kernel, n, sections, D, FF), out_s...]
    all_to_all x2 -> x0, waiting for transfers between devices: 102 us -> none  [the longest x1 52 us: shards(): lax.all_to_all(mixed, 'seq', split_axis=1, concat_axis=0, tiled=True)]
    all_gather x3 -> x0, waiting for transfers between devices: 34.9 us -> none  [the longest x1 34.9 us: shards(): lax.all_gather(contracting_diagonal_matrix[0], 'seq', axis=0, tiled=True)]
    dot_general x4 -> x0, matrix products: 20.1 us -> none  [the longest x1 9.75 us: shards(): jnp.einsum('tkf,kfe->tke', hidden, down_all.reshape(NB, FF // NB, D // NB...]
    ppermute x1 -> x0, waiting for transfers between devices: 17.4 us -> none  [from_behind(): lax.ppermute(value, axis, [(i, (i + by) % size) for i in range(size)])]
    convert_element_type x4 -> x0, local copies, waits for them, and re-layouts: 13.9 us -> none  [the longest x1 5.81 us: shards(): mixed = jnp.einsum('aob,abc->aoc', intragroup_mixing_matrix[0], normed, p...]
    all_to_all x2 -> x0, starting transfers between devices: 12.9 us -> none  [the longest x1 7.12 us: shards(): lax.all_to_all(turned, 'seq', split_axis=0, concat_axis=1, tiled=True)]
    unnamed x3 -> x0, other arithmetic: 12 us -> none
  transfers between devices with their start and end apart: 6 -> 0, of which waited for: 4 -> 0; matrix products, arithmetic and copies ran while one was open for 21% -> 0% of each run, Pallas kernels for 0% -> 0%
where the time goes in v1:
time: 126 us; the launch traced here: 125 us
  Pallas kernels  117 us (93%)
  local copies, waits for them, and re-layouts  8.67 us (7%)
    pallas_call x1, Pallas kernels, shards(): pl.pallas_call(functools.partial(layer_kernel, n, sections, D, FF), out_s...  117 us
    unnamed x15, local copies, waits for them, and re-layouts  7.86 us

profile of v1, /device:TPU:11, one launch (start us, length us, event | category | flops | bytes accessed | tf_op | source)
XLA Modules:
  0.0 125.4 jit_solution(12778819144254044305)
XLA Ops:
  0.0 0.0 copy-start
  0.0 0.7 copy-done
  0.7 0.8 copy.10
  1.5 0.0 copy-start.1
  1.5 1.4 %copy-done.1 = bf16[1,512,1536]{2,1,0:T(8,128)(2,1)S(1)} copy-done((bf16[1,512,1536]{2,1,0:T(8,128)(2,1)S(1)}, bf16[1,512,1536]{2,1,0:T(8,128)(2,1)}, u32[]{:S(2)}) %copy-start.1) | copy-done | bytes 1572888
  2.9 0.0 copy-start.2
  2.9 1.0 copy-done.2
  4.0 0.0 copy-start.3
  4.0 1.0 copy-done.3
  4.9 0.0 copy-start.4
  4.9 1.0 copy-done.4
  5.9 0.0 copy-start.5
  5.9 1.0 copy-done.5
  6.9 0.0 copy-start.6
  6.9 0.7 copy-done.6
  7.5 116.7 %encoder_layer.1 = bf16[512,1536]{1,0:T(8,128)(2,1)S(1)} custom-call(bf16[512,1536]{1,0:T(8,128)(2,1)S(1)} %bitcast.8, bf16[512,512]{1,0:T(8,128)(2,1)S(1)} %bitcast.9, bf16[64,128]{1,0:T(8,128)(2,1)S(1)} %pad.4.w_ref, f32[1,1536]{1,0:T(1,128)S(1)} %copy-done.6, bf16[192,768]{1,0:T(8,128)(2,1)S(1)} %bitcast.10, bf16[192,768]{1,0:T(8,128)(2,1)S(1)} %bitcast.11, ...), custom_call_target="tpu_custom_call" | custom-call | tf_op jit(solution)/shard_map/encoder_layer/pallas_call | solution.py:368
  124.2 1.1 copy.12
  (2 shorter events, 0.0 us)
Async XLA Ops:
  0.0 0.7 copy-start
  1.5 1.4 %copy-start.1 = (bf16[1,512,1536]{2,1,0:T(8,128)(2,1)S(1)}, bf16[1,512,1536]{2,1,0:T(8,128)(2,1)}, u32[]{:S(2)}) copy-start(bf16[1,512,1536]{2,1,0:T(8,128)(2,1)} %param.8) | copy-start | bytes 4718596
  2.9 1.0 copy-start.2
  4.0 1.0 copy-start.3
  4.9 1.0 copy-start.4
  5.9 1.0 copy-start.5
  6.9 0.7 copy-start.6

commit v2 on v1

--- a/solution.py
+++ b/solution.py
@@ -17,8 +17,9 @@
 
 def layer_kernel(
     n, sections, D, FF,
-    x_ref, a_ref, w_ref, g1_ref, gate_ref, up_ref, down_ref, g2_ref,
+    x_in, a_in, w_ref, g1_in, gate_ref, up_ref, down_ref, g2_in,
     out_ref,
+    x_ref, a_ref, g1_ref, g2_ref, ls,
     normed, mixed, xr, mr, w2, w3, wg, wu, wd, merged, st, outs,
     xs, xrs, ms, mrs, os_, ors, ws, wrs, ts, trs, vs, vrs,
 ):
@@ -33,6 +34,17 @@
     after = (sec + 1) % sections
     before = (sec + sections - 1) % sections
 
+    loads = [
+        pltpu.make_async_copy(x_in, x_ref, ls.at[0]),
+        pltpu.make_async_copy(a_in, a_ref, ls.at[1]),
+        pltpu.make_async_copy(g1_in, g1_ref, ls.at[2]),
+        pltpu.make_async_copy(
+            g2_in.at[:, pl.ds(pl.multiple_of(k * FB, FB), FB)], g2_ref, ls.at[3]
+        ),
+    ]
+    for load in loads:
+        load.start()
+
     barrier = pltpu.get_barrier_semaphore()
 
     def greet(j, carry):
@@ -171,6 +183,8 @@
         )
 
     pl.semaphore_wait(barrier, 3 * n - 1)
+    for load in loads:
+        load.wait()
 
     for b in range(NB):
         to = b * q + me // NB
@@ -270,10 +284,11 @@
 
             lax.fori_loop(0, r // T, tile, 0)
             v = merged[c]
-            st[c, k] = lax.dot_general(
+            sums = lax.dot_general(
                 jnp.ones((8, FB), jnp.float32), v * v, (((1,), (1,)), ((), ())),
                 precision=lax.Precision.HIGHEST, preferred_element_type=jnp.float32,
             )
+            st[c, k] = sums[0:1]
             for d in range(1, NB):
                 stat_copy(c, d).start()
 
@@ -295,7 +310,8 @@
             for d in range(1, NB):
                 stat_arrival(p, d).wait_recv()
             total = (st[p, 0] + st[p, 1]) + (st[p, 2] + st[p, 3])
-            scale = jnp.transpose(lax.rsqrt(total * (1.0 / D) + EPS))[:, 0:1]
+            scale = lax.rsqrt(total * (1.0 / D) + EPS)
+            scale = jnp.transpose(jnp.broadcast_to(scale, (8, n * r)))[:, 0:1]
             half = n * r // 2
             for t in range(2):
                 rows = slice(t * half, (t + 1) * half)
@@ -359,18 +375,20 @@
     flat = across[0].reshape(B1 // n, n * n)
     lanes = max(n * n, 128)
     flat = jnp.pad(flat, ((0, 0), (0, lanes - n * n)))
-    k = lax.axis_index("seq") // q
-    gain_two = lax.dynamic_slice(gain_two, (0, k * FB), (1, FB))
-    vmem = pl.BlockSpec(memory_space=pltpu.VMEM)
     anywhere = pl.BlockSpec(memory_space=pl.ANY)
     dma = pltpu.SemaphoreType.DMA
     bf, f32 = jnp.bfloat16, jnp.float32
     out = pl.pallas_call(
         functools.partial(layer_kernel, n, sections, D, FF),
         out_shape=jax.ShapeDtypeStruct((B1, D), bf),
-        in_specs=[vmem, vmem, anywhere, vmem, anywhere, anywhere, anywhere, vmem],
+        in_specs=[anywhere] * 8,
         out_specs=anywhere,
         scratch_shapes=[
+            pltpu.VMEM((B1, D), bf),
+            pltpu.VMEM((B1, B1), bf),
+            pltpu.VMEM((1, D), f32),
+            pltpu.VMEM((1, FB), f32),
+            dma((4,)),
             pltpu.VMEM((B1, D), bf),
             pltpu.VMEM((B1, D), bf),
             pltpu.VMEM((CHUNKS, n * r, FB), bf),
@@ -381,7 +399,7 @@
             pltpu.VMEM((FB, FH), bf),
             pltpu.VMEM((FH, FB), bf),
             pltpu.VMEM((CHUNKS, n * r, FB), f32),
-            pltpu.VMEM((CHUNKS, NB, 8, n * r), f32),
+            pltpu.VMEM((CHUNKS, NB, 1, n * r), f32),
             pltpu.VMEM((CHUNKS, n * r, FB), bf),
             dma((CHUNKS, n)), dma((CHUNKS, n)),
             dma((CHUNKS, n)), dma((CHUNKS, n)),
@@ -391,7 +409,7 @@
             dma((NB,)), dma((NB,)),
         ],
         compiler_params=pltpu.CompilerParams(
-            collective_id=0, has_side_effects=True, vmem_limit_bytes=48 * 1024 * 1024
+            collective_id=0, has_side_effects=True, vmem_limit_bytes=60 * 1024 * 1024
         ),
         name="encoder_layer",
     )(pending[0], along[0, 0], flat, gain_one, gate[0], up[0], down[0], gain_two)

time: 126 us -> 117 us (0.929)
  Pallas kernels: 117 us -> 112 us
  local copies, waits for them, and re-layouts: 8.67 us -> 4.08 us
    unnamed x15 -> x1, local copies, waits for them, and re-layouts: 7.86 us -> 2.65 us
    pallas_call x1, Pallas kernels: 117 us -> 112 us  [shards(): pl.pallas_call(functools.partial(layer_kernel, n, sections, D, FF), out_s...]
where the time goes in v2:
time: 117 us; the launch traced here: 116 us
  Pallas kernels  112 us (96%)
  local copies, waits for them, and re-layouts  4.08 us (3%)
    pallas_call x1, Pallas kernels, shards(): pl.pallas_call(functools.partial(layer_kernel, n, sections, D, FF), out_s...  112 us
    unnamed x1, local copies, waits for them, and re-layouts  2.65 us

profile of v2, /device:TPU:11, one launch (start us, length us, event | category | flops | bytes accessed | tf_op | source)
XLA Modules:
  0.0 116.4 jit_solution(17611427927496192059)
XLA Ops:
  0.0 0.8 copy.10
  0.8 0.6 pad.4.w_ref
  1.4 112.3 %encoder_layer.1 = bf16[512,1536]{1,0:T(8,128)(2,1)} custom-call(bf16[512,1536]{1,0:T(8,128)(2,1)} %bitcast.8, bf16[512,512]{1,0:T(8,128)(2,1)} %bitcast.9, bf16[64,128]{1,0:T(8,128)(2,1)} %pad.4.w_ref, f32[1,1536]{1,0:T(1,128)} %g1_in.1, bf16[192,768]{1,0:T(8,128)(2,1)} %bitcast.10, bf16[192,768]{1,0:T(8,128)(2,1)} %bitcast.11, bf16[384,384]{1,0:T(8,128)(2,1)} %bitcast.12, ...), custom_call_target="tpu_custom_call" | custom-call | tf_op jit(solution)/shard_map/encoder_layer/pallas_call | solution.py:381
  113.7 2.7 %copy.12 = bf16[1,512,1536]{2,1,0:T(8,128)(2,1)} copy(bf16[1,512,1536]{2,1,0:T(8,128)(2,1)} %bitcast.7) | data formatting | bytes 3145728

commit v3 on v2

--- a/solution.py
+++ b/solution.py
@@ -86,11 +86,15 @@
         return pltpu.make_async_copy(block_of(src, c, me), slot(land, c, me), recv.at[c, me])
 
     def start_chunk(src, land, send, recv, c):
-        def one(d, carry):
-            spread(src, land, send, recv, c, (me + d) % n).start()
-            return carry
-
-        lax.fori_loop(1, n, one, 0)
+        for dk in (2, 1, 3, 0):
+
+            def one(dh, carry):
+                j = (k + dk) % NB * q + (h + dh) % q
+                spread(src, land, send, recv, c, j).start()
+                return carry
+
+            lax.fori_loop(1 if dk == 0 else 0, q, one, 0)
+
         keep(src, land, recv, c).start()
 
     def await_chunk(src, land, send, recv, c):
@@ -183,21 +187,21 @@
         )
 
     pl.semaphore_wait(barrier, 3 * n - 1)
+    for b in range(NB):
+        to = b * q + me // NB
+
+        @pl.when(to != me)
+        def _():
+            across_copy(b).start()
+
+        @pl.when(to == me)
+        def _():
+            across_keep().start()
+
+    start_chunk(x_in, xr, xs, xrs, 0)
+
     for load in loads:
         load.wait()
-
-    for b in range(NB):
-        to = b * q + me // NB
-
-        @pl.when(to != me)
-        def _():
-            across_copy(b).start()
-
-        @pl.when(to == me)
-        def _():
-            across_keep().start()
-
-    start_chunk(x_ref, xr, xs, xrs, 0)
 
     def norm_rows(i, carry):
         rows = pl.ds(pl.multiple_of(i * 64, 64), 64)
@@ -220,7 +224,7 @@
         weight_keep(i).start()
     for c in range(1, AHEAD):
         start_chunk(mixed, mr, ms, mrs, c)
-        start_chunk(x_ref, xr, xs, xrs, c)
+        start_chunk(x_in, xr, xs, xrs, c)
 
     for i in range(NB):
         come = h * NB + i
@@ -276,7 +280,7 @@
         @pl.when(c < CHUNKS)
         def _():
             await_chunk(mixed, mr, ms, mrs, c)
-            await_chunk(x_ref, xr, xs, xrs, c)
+            await_chunk(x_in, xr, xs, xrs, c)
 
             def tile(i, carry):
                 turn_tile(c, i)
@@ -295,7 +299,7 @@
         @pl.when(c + AHEAD < CHUNKS)
         def _():
             start_chunk(mixed, mr, ms, mrs, c + AHEAD)
-            start_chunk(x_ref, xr, xs, xrs, c + AHEAD)
+            start_chunk(x_in, xr, xs, xrs, c + AHEAD)
 
         @pl.when(c == 1)
         def _():
@@ -346,7 +350,7 @@
     def drain(c, carry):
         def one(d, carry):
             j = (me + d) % n
-            spread(x_ref, xr, xs, xrs, c, j).wait_send()
+            spread(x_in, xr, xs, xrs, c, j).wait_send()
             spread(mixed, mr, ms, mrs, c, j).wait_send()
             return carry
 

time: 117 us -> 116 us (level)
  no operation moved by 1% of the time
where the time goes in v3:
time: 116 us
  Pallas kernels  112 us (97%)
  local copies, waits for them, and re-layouts  4.08 us (4%)
    pallas_call x1, Pallas kernels, shards(): pl.pallas_call(functools.partial(layer_kernel, n, sections, D, FF), out_s...  112 us
    unnamed x1, local copies, waits for them, and re-layouts  2.65 us

profile of v3, /device:TPU:11, one launch (start us, length us, event | category | flops | bytes accessed | tf_op | source)
XLA Modules:
  0.0 116.1 jit_solution(16514431257792168269)
XLA Ops:
  0.0 0.8 copy.10
  0.8 0.6 pad.4.w_ref
  1.4 112.0 %encoder_layer.1 = bf16[512,1536]{1,0:T(8,128)(2,1)} custom-call(bf16[512,1536]{1,0:T(8,128)(2,1)} %bitcast.8, bf16[512,512]{1,0:T(8,128)(2,1)} %bitcast.9, bf16[64,128]{1,0:T(8,128)(2,1)} %pad.4.w_ref, f32[1,1536]{1,0:T(1,128)} %g1_in.1, bf16[192,768]{1,0:T(8,128)(2,1)} %bitcast.10, bf16[192,768]{1,0:T(8,128)(2,1)} %bitcast.11, bf16[384,384]{1,0:T(8,128)(2,1)} %bitcast.12, ...), custom_call_target="tpu_custom_call" | custom-call | tf_op jit(solution)/shard_map/encoder_layer/pallas_call | solution.py:385
  113.5 2.7 %copy.12 = bf16[1,512,1536]{2,1,0:T(8,128)(2,1)} copy(bf16[1,512,1536]{2,1,0:T(8,128)(2,1)} %bitcast.7) | data formatting | bytes 3145728
